TPU v7x, 32 devices: a whole 2x2x4 slice. The times are simulated.
32 devices in a mesh: groups: 2 (over y), frame: 8 (over z, x), head: 2 (over core).
Axes of the slice: x: 2, y: 2, z: 4, core: 2. Of those that a mesh axis runs over, the one named last changes fastest.
Arguments:
- head_queries: bfloat16 [4096, 1536], P(('groups', 'frame'), 'head'), parts along dimension 0, may hold values from -10 to 10
- head_keys: bfloat16 [4096, 1536], P(('groups', 'frame'), 'head'), parts along dimension 0, may hold values from -10 to 10
- head_values: bfloat16 [4096, 1536], P(('groups', 'frame'), 'head'), parts along dimension 0, may hold values from -18 to 18
- out_weight: bfloat16 [1536, 3072], P('head', 'frame'), may hold values from -0.15625 to 0.15625
- head_class: int32 [12], P('head'), may hold values from 0 to 1, as said below
- block_lists: int32 [12, 16, 4, 2], P('head', ('groups', 'frame')), parts along dimension 1, may hold values from 0 to 3, as said below
- block_counts: int32 [12, 16, 4], P('head', ('groups', 'frame')), parts along dimension 1, may hold values from 1 to 2, as said below
Outputs:
- projected: bfloat16 [4096, 3072], P(('groups', 'frame', 'head')), parts along dimension 0
There are 2 independent parts, one for each index of `groups`. A program takes and returns all parts, laid end to end along the dimension named above; an argument that names none is the same for every part. Nothing has to cross between parts.
Inputs may be any that keep to these rules, and one draw needn't show every extreme that they name: `head_class`: for each j from 0 to 1, exactly half of the heads j * 6 to (j + 1) * 6 - 1 are temporal. block_lists[h, g, b, 0] equals b, and the entries of one list are distinct. `block_counts`: for each head and sequence some query block uses all 2 entries.
All inputs are finite; a program needn't handle non-finite values.
Results may differ from a plain program's by a relative error of at most 0.0062.
Values may be sent and summed in bfloat16 or wider, within the bound.
No kernel may reach another device: no remote copies, remote signals or barrier semaphores. Data moves between devices by JAX's collectives and lax.ppermute only.
A program may use at most 64 MiB of HBM per device.

v0:
```python
import jax
import jax.numpy as jnp
from jax import lax
from jax.sharding import PartitionSpec as P


def dense_head(queries_h, keys_h, values_h, block_ids, counts):
    block_count = block_ids.shape[0]
    listed_most = block_ids.shape[1]
    block_rows = queries_h.shape[0] // block_count
    usable = jnp.arange(listed_most)[None, :] < counts[:, None]
    linked = jnp.any(
        usable[:, :, None] & (block_ids[:, :, None] == jnp.arange(block_count)[None, None, :]),
        axis=1,
    )
    allowed = jnp.repeat(jnp.repeat(linked, block_rows, axis=0), block_rows, axis=1)
    scores = jnp.dot(queries_h, keys_h.T, preferred_element_type=jnp.float32) * queries_h.shape[
        1
    ] ** (-0.5)
    scores = jnp.where(allowed, scores, -jnp.inf)
    row_max = jnp.max(scores, axis=1, keepdims=True)
    weights = jnp.exp(scores - row_max)
    denominator = jnp.sum(weights, axis=1, keepdims=True)
    rounded = weights.astype(jnp.bfloat16)
    result = jnp.dot(rounded, values_h, preferred_element_type=jnp.float32) / denominator
    return result.astype(jnp.bfloat16)


def attend_heads(queries_h, keys_h, values_h, block_ids, counts):

    def single(inputs):
        return dense_head(*inputs)

    stacked = lax.map(
        single,
        (
            queries_h.transpose(1, 0, 2),
            keys_h.transpose(1, 0, 2),
            values_h.transpose(1, 0, 2),
            block_ids,
            counts,
        ),
    )
    return stacked.transpose(1, 0, 2)


def on_device(
    head_queries, head_keys, head_values, out_weight, head_class, block_lists, block_counts
):
    pixels = head_queries.shape[0]
    local_heads = head_class.shape[0]
    half_heads = local_heads // 2
    head_width = head_queries.shape[1] // local_heads
    groups = lax.axis_size("frame")
    head_order = jnp.argsort(head_class, stable=True)
    inverse = jnp.argsort(head_order)
    spatial_ids = head_order[:half_heads]
    temporal_ids = head_order[half_heads:]
    block_ids = block_lists[:, 0]
    counts = block_counts[:, 0]

    def split_heads(tensor, chosen):
        return jnp.take(tensor.reshape(pixels, local_heads, head_width), chosen, axis=1)

    temporal_q = split_heads(head_queries, temporal_ids).reshape(1, pixels, half_heads * head_width)
    temporal_k = split_heads(head_keys, temporal_ids).reshape(1, pixels, half_heads * head_width)
    temporal_v = split_heads(head_values, temporal_ids).reshape(1, pixels, half_heads * head_width)
    arrived = (
        lax.all_to_all(temporal_q, "frame", split_axis=1, concat_axis=0, tiled=True),
        lax.all_to_all(temporal_k, "frame", split_axis=1, concat_axis=0, tiled=True),
        lax.all_to_all(temporal_v, "frame", split_axis=1, concat_axis=0, tiled=True),
    )
    spatial = attend_heads(
        split_heads(head_queries, spatial_ids),
        split_heads(head_keys, spatial_ids),
        split_heads(head_values, spatial_ids),
        block_ids[spatial_ids],
        counts[spatial_ids],
    )
    temporal = attend_heads(
        arrived[0].reshape(pixels, half_heads, head_width),
        arrived[1].reshape(pixels, half_heads, head_width),
        arrived[2].reshape(pixels, half_heads, head_width),
        block_ids[temporal_ids],
        counts[temporal_ids],
    )
    returned = lax.all_to_all(
        temporal.reshape(groups, pixels // groups, half_heads * head_width),
        "frame",
        split_axis=0,
        concat_axis=1,
        tiled=True,
    )
    joined = jnp.concatenate([spatial, returned.reshape(pixels, half_heads, head_width)], axis=1)
    attended = jnp.take(joined, inverse, axis=1).reshape(pixels, local_heads * head_width)
    partial_out = jnp.dot(
        attended,
        lax.all_gather(out_weight, "frame", axis=1, tiled=True),
        preferred_element_type=jnp.float32,
    )
    projected = lax.psum_scatter(
        partial_out.astype(jnp.bfloat16), "head", scatter_dimension=0, tiled=True
    )
    return projected


def solution(mesh):
    placed = (
        P(("groups", "frame"), "head"),
        P(("groups", "frame"), "head"),
        P(("groups", "frame"), "head"),
        P("head", "frame"),
        P("head"),
        P("head", ("groups", "frame"), None, None),
        P("head", ("groups", "frame"), None),
    )
    return jax.shard_map(
        on_device,
        mesh=mesh,
        in_specs=placed,
        out_specs=P(("groups", "frame", "head"), None),
        check_vma=False,
    )
```

profile of v0, /device:TPU:0, one launch (start us, length us, event | category | flops | bytes accessed | tf_op | source)
XLA Modules:
  0.0 125.5 jit_solution(15839549879468988712)
XLA Ops:
  6.5 0.7 all-gather.2.cloned.1.call-update
  7.3 1.6 %sort.34 = (s32[6]{0:T(128)}, s32[6]{0:T(128)S(1)}) sort(s32[6]{0:T(128)} %param.17, s32[6]{0:T(128)S(1)} %iota.30), dimensions={0}, to_apply=%region_0.0 | sort | flops 18 | bytes 96 | tf_op jit(solution)/shard_map/jit(argsort)/sort | solution.py:55
  9.0 1.2 copy.101
  10.4 1.2 copy.103
  11.8 0.6 gather_fusion.5
  13.0 0.6 gather_fusion.8
  13.6 0.6 gather_fusion.9
  14.6 0.6 gather_fusion.7
  15.2 0.6 gather_fusion.10
  16.6 0.6 broadcast.192
  17.2 1.8 %reduce = bf16[256,384]{1,0:T(8,128)(2,1)S(1)} reduce(bf16[256,1,384]{2,1,0:T(2,128)(2,1)S(1)} %bitcast.137, bf16[]{:T(256)} %broadcast.192), dimensions={1}, to_apply=%bitcast.83.reduce_sub_computation | reduce | bytes 393218
  19.0 0.7 reshape.257
  19.7 7.3 %all-to-all-start = ((bf16[8,2,6144]{2,1,0:T(2,128)(2,1)}), bf16[8,2,6144]{2,1,0:T(2,128)(2,1)S(1)}, u32[]{:S(2)}, u32[]{:S(2)}) async-start(bf16[8,2,6144]{2,1,0:T(2,128)(2,1)} %reshape.257), calls=%async_computation | async-start | bytes 393216 | tf_op jit(solution)/shard_map/all_to_all | solution.py:69
  27.6 1.8 %reduce.1 = bf16[256,384]{1,0:T(8,128)(2,1)S(1)} reduce(bf16[256,1,384]{2,1,0:T(2,128)(2,1)S(1)} %bitcast.139, bf16[]{:T(256)} %broadcast.192), dimensions={1}, to_apply=%bitcast.85.reduce_sub_computation | reduce | bytes 393218
  29.5 0.7 reshape.259
  30.2 8.7 %all-to-all-done = bf16[8,2,6144]{2,1,0:T(2,128)(2,1)S(1)} async-done(((bf16[8,2,6144]{2,1,0:T(2,128)(2,1)}), bf16[8,2,6144]{2,1,0:T(2,128)(2,1)S(1)}, u32[]{:S(2)}, u32[]{:S(2)}) %all-to-all-start) | async-done | bytes 196640 | tf_op jit(solution)/shard_map/all_to_all | solution.py:69
  38.9 4.6 %all-to-all-start.1 = ((bf16[8,2,6144]{2,1,0:T(2,128)(2,1)}), bf16[8,2,6144]{2,1,0:T(2,128)(2,1)S(1)}, u32[]{:S(2)}, u32[]{:S(2)}) async-start(bf16[8,2,6144]{2,1,0:T(2,128)(2,1)} %reshape.259), calls=%async_computation.1 | async-start | bytes 393216 | tf_op jit(solution)/shard_map/all_to_all | solution.py:70
  45.5 1.8 %reduce.2 = bf16[256,384]{1,0:T(8,128)(2,1)S(1)} reduce(bf16[256,1,384]{2,1,0:T(2,128)(2,1)S(1)} %bitcast.138, bf16[]{:T(256)} %broadcast.192), dimensions={1}, to_apply=%bitcast.87.reduce_sub_computation | reduce | bytes 393218
  47.3 0.7 reshape.261
  48.1 5.5 %all-to-all-done.1 = bf16[8,2,6144]{2,1,0:T(2,128)(2,1)S(1)} async-done(((bf16[8,2,6144]{2,1,0:T(2,128)(2,1)}), bf16[8,2,6144]{2,1,0:T(2,128)(2,1)S(1)}, u32[]{:S(2)}, u32[]{:S(2)}) %all-to-all-start.1) | async-done | bytes 196640 | tf_op jit(solution)/shard_map/all_to_all | solution.py:70
  53.6 3.4 %all-to-all-start.2 = ((bf16[8,2,6144]{2,1,0:T(2,128)(2,1)}), bf16[8,2,6144]{2,1,0:T(2,128)(2,1)S(1)}, u32[]{:S(2)}, u32[]{:S(2)}) async-start(bf16[8,2,6144]{2,1,0:T(2,128)(2,1)} %reshape.261), calls=%async_computation.2 | async-start | bytes 393216 | tf_op jit(solution)/shard_map/all_to_all | solution.py:71
  57.0 3.0 %while.20 = (s32[]{:T(128)}, bf16[3,256,128]{2,1,0:T(8,128)(2,1)S(1)}, s32[3,4]{1,0:T(4,128)S(1)}, s32[3,4,2]{1,2,0:T(2,128)S(1)}, bf16[3,256,128]{2,1,0:T(8,128...) while((s32[]{:T(128)}, bf16[3,256,128]{2,1,0:T(8,128)(2,1)S(1)}, ...), condition=%wide.region_6.8_spmd, body=%wide.region_2.7_spmd.sunk | while | flops 34078296 | bytes 1191229 | solution.py:34
  61.2 0.9 sort.35
  63.4 7.5 %all-to-all-done.2 = bf16[8,2,6144]{2,1,0:T(2,128)(2,1)S(1)} async-done(((bf16[8,2,6144]{2,1,0:T(2,128)(2,1)}), bf16[8,2,6144]{2,1,0:T(2,128)(2,1)S(1)}, u32[]{:S(2)}, u32[]{:S(2)}) %all-to-all-start.2) | async-done | bytes 196640 | tf_op jit(solution)/shard_map/all_to_all | solution.py:71
  71.5 3.1 %while.21 = (s32[]{:T(128)}, bf16[3,256,128]{2,1,0:T(8,128)(2,1)S(1)}, s32[3,4]{1,0:T(4,128)S(1)}, s32[3,4,2]{1,2,0:T(2,128)S(1)}, bf16[3,256,128]{1,2,0:T(8,128...) while((s32[]{:T(128)}, ...), condition=%wide.region_11.13_spmd, body=%wide.region_7.12_spmd.sunk | while | flops 34078296 | bytes 1191229 | solution.py:34
  74.8 0.8 reshape.144
  75.7 3.4 %all-to-all-start.3 = ((bf16[8,32,384]{2,1,0:T(8,128)(2,1)}), bf16[8,32,384]{2,1,0:T(8,128)(2,1)S(1)}, u32[]{:S(2)}, u32[]{:S(2)}) async-start(bf16[8,32,384]{2,1,0:T(8,128)(2,1)} %reshape.144), calls=%async_computation.3 | async-start | bytes 393216 | tf_op jit(solution)/shard_map/all_to_all | solution.py:87
  79.3 9.9 %all-to-all-done.3 = bf16[8,32,384]{2,1,0:T(8,128)(2,1)S(1)} async-done(((bf16[8,32,384]{2,1,0:T(8,128)(2,1)}), bf16[8,32,384]{2,1,0:T(8,128)(2,1)S(1)}, u32[]{:S(2)}, u32[]{:S(2)}) %all-to-all-start.3) | async-done | bytes 196640 | tf_op jit(solution)/shard_map/all_to_all | solution.py:87
  89.3 0.6 gather_fusion.4
  90.3 14.7 %all-gather.2.cloned.1.call-done = bf16[768,3072]{1,0:T(8,128)(2,1)} async-done(((bf16[768,384]{1,0:T(8,128)(2,1)}), bf16[768,3072]{1,0:T(8,128)(2,1)}) %all-gather.2.cloned.1.call-update) | async-done | bytes 4718608 | tf_op jit(solution)/shard_map/all_gather | solution.py:98
  104.9 4.9 %convolution_convert_fusion = bf16[256,3072]{1,0:T(8,128)(2,1)} fusion(bf16[256,768]{0,1:T(8,128)(2,1)S(1)} %bitcast_select_fusion, bf16[768,3072]{1,0:T(8,128)(2,1)} %all-gather.2.cloned.1.call-done), kind=kOutput, calls=%fused_computation.63 | convolution fusion | flops 1208745984 | bytes 6684672 | tf_op jit(solution)/shard_map/dot_general | solution.py:96
  109.9 8.7 %reduce-scatter.2.cloned.1.call-done = bf16[128,3072]{1,0:T(8,128)(2,1)} async-done(((bf16[256,3072]{1,0:T(8,128)(2,1)}), bf16[128,3072]{1,0:T(8,128)(2,1)}) %reduce-scatter.2.cloned.1.call-update) | async-done | bytes 786448 | tf_op jit(solution)/shard_map/reduce_scatter | solution.py:101
  (117 shorter events, 14.5 us)
Async XLA Ops:
  6.5 7.6 %copy-start = (bf16[256,768]{1,0:T(8,128)(2,1)S(1)}, bf16[256,768]{1,0:T(8,128)(2,1)}, u32[]{:S(2)}) copy-start(bf16[256,768]{1,0:T(8,128)(2,1)} %param.15) | copy-start | bytes 1179652
  6.5 98.4 %all-gather.2.cloned.1.call-start = ((), (), s32[]{:S(2)}) async-start(), calls=%async_computation.5 | async-start | bytes 5308416 | tf_op jit(solution)/shard_map/all_gather | solution.py:98
  14.2 29.4 %copy-start.1 = (s32[6,1,4,2]{0,3,2,1:T(2,128)S(1)}, s32[6,1,4,2]{0,3,2,1:T(2,128)}, u32[]{:S(2)}) copy-start(s32[6,1,4,2]{0,3,2,1:T(2,128)} %param.18) | copy-start | bytes 580
  14.2 30.0 %copy-start.2 = (s32[6,1,4]{0,2,1:T(4,128)S(1)}, s32[6,1,4]{0,2,1:T(4,128)}, u32[]{:S(2)}) copy-start(s32[6,1,4]{0,2,1:T(4,128)} %param.19) | copy-start | bytes 292
  19.7 19.2 %all-to-all-start = ((bf16[8,2,6144]{2,1,0:T(2,128)(2,1)}), bf16[8,2,6144]{2,1,0:T(2,128)(2,1)S(1)}, u32[]{:S(2)}, u32[]{:S(2)}) async-start(bf16[8,2,6144]{2,1,0:T(2,128)(2,1)} %reshape.257), calls=%async_computation | async-start | bytes 393216 | tf_op jit(solution)/shard_map/all_to_all | solution.py:69
  38.9 14.7 %all-to-all-start.1 = ((bf16[8,2,6144]{2,1,0:T(2,128)(2,1)}), bf16[8,2,6144]{2,1,0:T(2,128)(2,1)S(1)}, u32[]{:S(2)}, u32[]{:S(2)}) async-start(bf16[8,2,6144]{2,1,0:T(2,128)(2,1)} %reshape.259), calls=%async_computation.1 | async-start | bytes 393216 | tf_op jit(solution)/shard_map/all_to_all | solution.py:70
  53.6 17.3 %all-to-all-start.2 = ((bf16[8,2,6144]{2,1,0:T(2,128)(2,1)}), bf16[8,2,6144]{2,1,0:T(2,128)(2,1)S(1)}, u32[]{:S(2)}, u32[]{:S(2)}) async-start(bf16[8,2,6144]{2,1,0:T(2,128)(2,1)} %reshape.261), calls=%async_computation.2 | async-start | bytes 393216 | tf_op jit(solution)/shard_map/all_to_all | solution.py:71
  75.7 13.5 %all-to-all-start.3 = ((bf16[8,32,384]{2,1,0:T(8,128)(2,1)}), bf16[8,32,384]{2,1,0:T(8,128)(2,1)S(1)}, u32[]{:S(2)}, u32[]{:S(2)}) async-start(bf16[8,32,384]{2,1,0:T(8,128)(2,1)} %reshape.144), calls=%async_computation.3 | async-start | bytes 393216 | tf_op jit(solution)/shard_map/all_to_all | solution.py:87
  79.1 39.5 %reduce-scatter.2.cloned.1.call-start = ((), (), s32[]{:S(2)}) async-start(), calls=%async_computation.6 | async-start | bytes 2359296 | tf_op jit(solution)/shard_map/reduce_scatter | solution.py:101
Sparse Core Ops, SparseCore 0:
  9.4 95.4 all-gather.1
  110.0 8.5 reduce-scatter.1
where the time goes:
time: 126 us; the launch traced here: 125 us
  waiting for transfers between devices  55.8 us (44%)
  local copies, waits for them, and re-layouts  19.5 us (15%)
  starting transfers between devices  18.7 us (15%)
  between operations  13.7 us (11%)
  other arithmetic  9.56 us (8%)
  matrix products  7.91 us (6%)
    all_gather x1, waiting for transfers between devices, on_device(): lax.all_gather(out_weight, 'frame', axis=1, tiled=True)  14.7 us
    all_to_all x1, waiting for transfers between devices, on_device(): lax.all_to_all(temporal.reshape(groups, pixels // groups, half_heads * he...  9.88 us
    reduce_scatter x1, waiting for transfers between devices, on_device(): lax.psum_scatter(partial_out.astype(jnp.bfloat16), 'head', scatter_dimens...  8.74 us
    all_to_all x1, waiting for transfers between devices, on_device(): lax.all_to_all(temporal_q, 'frame', split_axis=1, concat_axis=0, tiled=True)  8.72 us
    all_to_all x1, waiting for transfers between devices, on_device(): lax.all_to_all(temporal_v, 'frame', split_axis=1, concat_axis=0, tiled=True)  7.5 us
    all_to_all x1, starting transfers between devices, on_device(): lax.all_to_all(temporal_q, 'frame', split_axis=1, concat_axis=0, tiled=True)  7.25 us
    unnamed x17, local copies, waits for them, and re-layouts  5.83 us
    unnamed x3, other arithmetic  5.54 us
  transfers between devices with their start and end apart: 6, of which 6 were waited for; matrix products, arithmetic and copies ran while one was open for 25% of the time, Pallas kernels for 0%

commit v1 on v0

--- a/solution.py
+++ b/solution.py
@@ -1,7 +1,34 @@
+import functools
 import jax
 import jax.numpy as jnp
 from jax import lax
 from jax.sharding import PartitionSpec as P
+
+
+def reach_pages(raw, array_dim):
+    n_shards = lax.axis_size("frame")
+    piece_now = range(n_shards)
+    local_out = map(lambda b: (b, (b + 1) % n_shards), piece_now)
+    arrivals = list(local_out)
+    w2 = range(n_shards)
+    piece_next = map(lambda b: (b, (b - 1) % n_shards), w2)
+    block_next, item_now = ([raw], [raw])
+    sheets = list(piece_next)
+    for _ in range(n_shards // 2):
+        block_next.append(lax.ppermute(block_next[-1], axis_name="frame", perm=arrivals))
+    c = 0
+    while c < (n_shards - 1) // 2:
+        item_now.append(lax.ppermute(item_now[-1], axis_name="frame", perm=sheets))
+        c = c + 1
+    new = jnp.roll(
+        jnp.concatenate([*block_next[::-1], *item_now[1:]], array_dim),
+        (lax.axis_index("frame") - n_shards // 2) * raw.shape[array_dim],
+        axis=array_dim,
+    )
+    return new
+
+
+connect_the_inputs = functools.partial(reach_pages, array_dim=1)
 
 
 def dense_head(queries_h, keys_h, values_h, block_ids, counts):
@@ -94,9 +121,7 @@
     joined = jnp.concatenate([spatial, returned.reshape(pixels, half_heads, head_width)], axis=1)
     attended = jnp.take(joined, inverse, axis=1).reshape(pixels, local_heads * head_width)
     partial_out = jnp.dot(
-        attended,
-        lax.all_gather(out_weight, "frame", axis=1, tiled=True),
-        preferred_element_type=jnp.float32,
+        attended, connect_the_inputs(out_weight), preferred_element_type=jnp.float32
     )
     projected = lax.psum_scatter(
         partial_out.astype(jnp.bfloat16), "head", scatter_dimension=0, tiled=True

time: 126 us -> 163 us (1.29)
  starting transfers between devices: 18.7 us -> 48.6 us
  waiting for transfers between devices: 55.8 us -> 30.9 us
  local copies, waits for them, and re-layouts: 19.5 us -> 39.5 us
  other arithmetic: 9.56 us -> 17.1 us
  matrix products: 7.91 us -> 11.3 us
    ppermute x0 -> x7, waiting for transfers between devices: none -> 17.5 us  [the longest x3 17.5 us: reach_pages(): item_now.append(lax.ppermute(item_now[-1], axis_name='frame', perm=sheets))]
    ppermute x0 -> x7, starting transfers between devices: none -> 16.2 us  [the longest x3 10.8 us: reach_pages(): item_now.append(lax.ppermute(item_now[-1], axis_name='frame', perm=sheets))]
    all_gather x1 -> x0, waiting for transfers between devices: 14.7 us -> none  [on_device(): lax.all_gather(out_weight, 'frame', axis=1, tiled=True)]
    all_to_all x1, starting transfers between devices: 4.62 us -> 14 us  [on_device(): lax.all_to_all(temporal_k, 'frame', split_axis=1, concat_axis=0, tiled=True)]
    all_to_all x1, waiting for transfers between devices: 9.88 us -> 0.65 us  [on_device(): lax.all_to_all(temporal.reshape(groups, pixels // groups, half_heads * he...]
    all_to_all x1, waiting for transfers between devices: 7.5 us -> 0.01 us  [on_device(): lax.all_to_all(temporal_v, 'frame', split_axis=1, concat_axis=0, tiled=True)]
    all_to_all x1, waiting for transfers between devices: 5.54 us -> 0.01 us  [on_device(): lax.all_to_all(temporal_k, 'frame', split_axis=1, concat_axis=0, tiled=True)]
    unnamed x17 -> x42, local copies, waits for them, and re-layouts: 5.83 us -> 11 us
  transfers between devices with their start and end apart: 6 -> 12, of which waited for: 6 -> 5; matrix products, arithmetic and copies ran while one was open for 25% -> 30% of each run, Pallas kernels for 0% -> 0%
where the time goes in v1:
time: 163 us; the launch traced here: 161 us
  starting transfers between devices  48.6 us (30%)
  local copies, waits for them, and re-layouts  39.5 us (24%)
  waiting for transfers between devices  30.9 us (19%)
  other arithmetic  17.1 us (10%)
  between operations  13.8 us (8%)
  matrix products  11.3 us (7%)
    ppermute x3, waiting for transfers between devices, reach_pages(): item_now.append(lax.ppermute(item_now[-1], axis_name='frame', perm=sheets))  17.5 us
    all_to_all x1, starting transfers between devices, on_device(): lax.all_to_all(temporal_k, 'frame', split_axis=1, concat_axis=0, tiled=True)  14 us
    unnamed x42, local copies, waits for them, and re-layouts  11 us
    ppermute x3, starting transfers between devices, reach_pages(): item_now.append(lax.ppermute(item_now[-1], axis_name='frame', perm=sheets))  10.8 us
    reduce_scatter x1, waiting for transfers between devices, on_device(): lax.psum_scatter(partial_out.astype(jnp.bfloat16), 'head', scatter_dimens...  8.8 us
    all_to_all x1, starting transfers between devices, on_device(): lax.all_to_all(temporal_q, 'frame', split_axis=1, concat_axis=0, tiled=True)  7.25 us
    all_to_all x1, starting transfers between devices, on_device(): lax.all_to_all(temporal_v, 'frame', split_axis=1, concat_axis=0, tiled=True)  6.69 us
    dot_general x6, matrix products, dense_head(): jnp.dot(rounded, values_h, preferred_element_type=jnp.float32) / denominator  6.54 us
  transfers between devices with their start and end apart: 12, of which 5 were waited for; matrix products, arithmetic and copies ran while one was open for 30% of the time, Pallas kernels for 0%

profile of v1, /device:TPU:0, one launch (start us, length us, event | category | flops | bytes accessed | tf_op | source)
XLA Modules:
  0.0 161.5 jit_solution(16343145466773676660)
XLA Ops:
  6.5 1.7 %sort.34 = (s32[6]{0:T(128)}, s32[6]{0:T(128)S(1)}) sort(s32[6]{0:T(128)} %param.17, s32[6]{0:T(128)S(1)} %iota.30), dimensions={0}, to_apply=%region_0.0 | sort | flops 18 | bytes 96 | tf_op jit(solution)/shard_map/jit(argsort)/sort | solution.py:82
  8.3 1.2 copy.101
  9.7 1.2 copy.103
  13.5 1.2 copy.105
  18.1 1.8 %reduce = bf16[256,384]{1,0:T(8,128)(2,1)S(1)} reduce(bf16[256,1,384]{2,1,0:T(2,128)(2,1)S(1)} %bitcast.136, bf16[]{:T(256)} %broadcast.192), dimensions={1}, to_apply=%bitcast.83.reduce_sub_computation | reduce | bytes 393218
  20.7 7.3 %all-to-all-start = ((bf16[8,2,6144]{2,1,0:T(2,128)(2,1)}), bf16[8,2,6144]{2,1,0:T(2,128)(2,1)S(1)}, u32[]{:S(2)}, u32[]{:S(2)}) async-start(bf16[8,2,6144]{2,1,0:T(2,128)(2,1)} %reshape.257), calls=%async_computation | async-start | bytes 393216 | tf_op jit(solution)/shard_map/all_to_all | solution.py:96
  28.0 2.0 %collective-permute-start = (bf16[768,384]{1,0:T(8,128)(2,1)S(1)}, bf16[768,384]{1,0:T(8,128)(2,1)S(1)}, u32[]{:S(2)}, u32[]{:S(2)}) collective-permute-start(bf16[768,384]{1,0:T(8,128)(2,1)S(1)} %copy-done), channel_id=1, source_target_pairs={{0,2},{2,4},{4,6},{6,8},{8,10},{10,12},{12,14},{14,0},{1,3},{3,5},... | collective-permute-start | bytes 1769480 | tf_op jit(solution)/shard_map/ppermute | solution.py:18
  30.6 1.8 %reduce.1 = bf16[256,384]{1,0:T(8,128)(2,1)S(1)} reduce(bf16[256,1,384]{2,1,0:T(2,128)(2,1)S(1)} %bitcast.138, bf16[]{:T(256)} %broadcast.192), dimensions={1}, to_apply=%bitcast.85.reduce_sub_computation | reduce | bytes 393218
  33.2 3.9 %all-to-all-done = bf16[8,2,6144]{2,1,0:T(2,128)(2,1)S(1)} async-done(((bf16[8,2,6144]{2,1,0:T(2,128)(2,1)}), bf16[8,2,6144]{2,1,0:T(2,128)(2,1)S(1)}, u32[]{:S(2)}, u32[]{:S(2)}) %all-to-all-start) | async-done | bytes 196640 | tf_op jit(solution)/shard_map/all_to_all | solution.py:96
  37.1 14.0 %all-to-all-start.1 = ((bf16[8,2,6144]{2,1,0:T(2,128)(2,1)}), bf16[8,2,6144]{2,1,0:T(2,128)(2,1)S(1)}, u32[]{:S(2)}, u32[]{:S(2)}) async-start(bf16[8,2,6144]{2,1,0:T(2,128)(2,1)} %reshape.259), calls=%async_computation.1 | async-start | bytes 393216 | tf_op jit(solution)/shard_map/all_to_all | solution.py:97
  51.1 4.7 %collective-permute-start.4 = (bf16[768,384]{1,0:T(8,128)(2,1)S(1)}, bf16[768,384]{1,0:T(8,128)(2,1)S(1)}, u32[]{:S(2)}, u32[]{:S(2)}) collective-permute-start(bf16[768,384]{1,0:T(8,128)(2,1)S(1)} %copy-done), channel_id=1, source_target_pairs={{0,14},{2,0},{4,2},{6,4},{8,6},{10,8},{12,10},{14,12},{1,15},{3,1}... | collective-permute-start | bytes 1769480 | tf_op jit(solution)/shard_map/ppermute | solution.py:21
  58.3 1.8 %reduce.2 = bf16[256,384]{1,0:T(8,128)(2,1)S(1)} reduce(bf16[256,1,384]{2,1,0:T(2,128)(2,1)S(1)} %bitcast.137, bf16[]{:T(256)} %broadcast.192), dimensions={1}, to_apply=%bitcast.87.reduce_sub_computation | reduce | bytes 393218
  60.9 6.7 %all-to-all-start.2 = ((bf16[8,2,6144]{2,1,0:T(2,128)(2,1)}), bf16[8,2,6144]{2,1,0:T(2,128)(2,1)S(1)}, u32[]{:S(2)}, u32[]{:S(2)}) async-start(bf16[8,2,6144]{2,1,0:T(2,128)(2,1)} %reshape.261), calls=%async_computation.2 | async-start | bytes 393216 | tf_op jit(solution)/shard_map/all_to_all | solution.py:98
  67.6 11.3 %while.20 = (s32[]{:T(128)}, bf16[3,256,128]{2,1,0:T(8,128)(2,1)S(1)}, s32[3,4]{1,0:T(4,128)}, s32[3,4,2]{1,2,0:T(2,128)S(1)}, bf16[3,256,128]{2,1,0:T(8,128)(2,...) while((s32[]{:T(128)}, bf16[3,256,128]{2,1,0:T(8,128)(2,1)S(1)}, ...), condition=%wide.region_6.8_spmd, body=%wide.region_2.7_spmd.sunk | while | flops 34078296 | bytes 1191229 | solution.py:61
  78.9 1.4 gather_fusion.3
  80.3 1.3 gather_fusion.2
  81.6 1.6 sort.35
  86.1 2.1 %collective-permute-start.2 = (bf16[768,384]{1,0:T(8,128)(2,1)S(1)}, bf16[768,384]{1,0:T(8,128)(2,1)S(1)}, u32[]{:S(2)}, u32[]{:S(2)}) collective-permute-start(bf16[768,384]{1,0:T(8,128)(2,1)S(1)} %collective-permute-done.1), channel_id=1, source_target_pairs={{0,2},{2,4},{4,6},{6,8},{8,10},{10,12},{12,14},{14,0},{1,3},{3,5},... | collective-permute-start | bytes 1769480 | tf_op jit(solution)/shard_map/ppermute | solution.py:18
  88.2 7.7 %while.21 = (s32[]{:T(128)}, bf16[3,256,128]{2,1,0:T(8,128)(2,1)S(1)}, s32[3,4]{1,0:T(4,128)}, s32[3,4,2]{1,2,0:T(2,128)S(1)}, bf16[3,256,128]{1,2,0:T(8,128)(2,...) while((s32[]{:T(128)}, bf16[3,256,128]{2,1,0:T(8,128)(2,1)S(1)}, ...), condition=%wide.region_11.13_spmd, body=%wide.region_7.12_spmd.sunk | while | flops 34078296 | bytes 1191229 | solution.py:61
  96.9 4.5 %all-to-all-start.3 = ((bf16[8,32,384]{2,1,0:T(8,128)(2,1)}), bf16[8,32,384]{2,1,0:T(8,128)(2,1)}, u32[]{:S(2)}, u32[]{:S(2)}) async-start(bf16[8,32,384]{2,1,0:T(8,128)(2,1)} %reshape.144), calls=%async_computation.3 | async-start | bytes 393216 | tf_op jit(solution)/shard_map/all_to_all | solution.py:114
  102.7 4.7 %collective-permute-start.5 = (bf16[768,384]{1,0:T(8,128)(2,1)S(1)}, bf16[768,384]{1,0:T(8,128)(2,1)S(1)}, u32[]{:S(2)}, u32[]{:S(2)}) collective-permute-start(bf16[768,384]{1,0:T(8,128)(2,1)S(1)} %collective-permute-done.4), channel_id=1, source_target_pairs={{0,14},{2,0},{4,2},{6,4},{8,6},{10,8},{12,10},{14,12},{1,15},{3,1}... | collective-permute-start | bytes 1769480 | tf_op jit(solution)/shard_map/ppermute | solution.py:21
  107.4 1.3 collective-permute-start.3
  109.4 1.7 %reshape.145 = bf16[256,3,128]{2,1,0:T(4,128)(2,1)} reshape(bf16[8,32,384]{2,1,0:T(8,128)(2,1)} %all-to-all-done.3) | data formatting | bytes 393216 | tf_op jit(solution)/shard_map/reshape | solution.py:121
  112.1 1.7 %pad_maximum_fusion = bf16[256,6,128]{2,0,1:T(8,128)(2,1)} fusion(bf16[256,3,128]{2,0,1:T(8,128)(2,1)S(1)} %copy.125, bf16[256,3,128]{2,0,1:T(8,128)(2,1)} %bitcast.142), kind=kLoop, calls=%fused_computation.66 | loop fusion | flops 196608 | bytes 786432 | tf_op jit(solution)/shard_map/concatenate | solution.py:121
  113.8 2.3 %gather_fusion.4 = bf16[6,256,128]{2,1,0:T(8,128)(2,1)} fusion(bf16[256,6,128]{2,0,1:T(8,128)(2,1)} %pad_maximum_fusion, s32[1024]{0:T(1024)S(1)} %pad_clamp_fusion), kind=kCustom, calls=%fused_computation.10 | custom fusion | bytes 786456 | tf_op jit(solution)/shard_map/jit(_take)/gather | solution.py:122
  116.1 1.9 %copy.126 = bf16[256,6,128]{0,2,1:T(8,128)(2,1)} copy(bf16[256,6,128]{2,0,1:T(8,128)(2,1)} %bitcast.129) | data formatting | bytes 786432 | tf_op jit(solution)/shard_map/jit(_take)/gather | solution.py:122
  119.2 6.7 %collective-permute-done.5 = bf16[768,384]{1,0:T(8,128)(2,1)S(1)} collective-permute-done((bf16[768,384]{1,0:T(8,128)(2,1)S(1)}, bf16[768,384]{1,0:T(8,128)(2,1)S(1)}, u32[]{:S(2)}, u32[]{:S(2)}) %collective-permute-start.5) | collective-permute-done | bytes 589856 | tf_op jit(solution)/shard_map/ppermute | solution.py:21
  125.9 1.4 collective-permute-start.6
  129.4 10.8 %collective-permute-done.6 = bf16[768,384]{1,0:T(8,128)(2,1)S(1)} collective-permute-done((bf16[768,384]{1,0:T(8,128)(2,1)S(1)}, bf16[768,384]{1,0:T(8,128)(2,1)S(1)}, u32[]{:S(2)}, u32[]{:S(2)}) %collective-permute-start.6) | collective-permute-done | bytes 589856 | tf_op jit(solution)/shard_map/ppermute | solution.py:21
  140.3 1.2 constant_dynamic-update-slice_fusion.7
  142.5 3.2 %fusion.42 = bf16[256,3072]{1,0:T(8,128)(2,1)} fusion(bf16[256,768]{0,1:T(8,128)(2,1)S(1)} %bitcast_select_fusion, bf16[768,6144]{1,0:T(8,128)(2,1)S(1)} %constant_dynamic-update-slice_fusion, s32[]{:T(128)S(6)} %select_n.50), kind=kOutput, calls=%fused_computation.65 | convolution fusion | flops 1208745984 | bytes 6684676 | tf_op jit(solution)/shard_map/dot_general | solution.py:123
  145.8 8.8 %reduce-scatter.2.cloned.1.call-done = bf16[128,3072]{1,0:T(8,128)(2,1)} async-done(((bf16[256,3072]{1,0:T(8,128)(2,1)}), bf16[128,3072]{1,0:T(8,128)(2,1)}) %reduce-scatter.2.cloned.1.call-update) | async-done | bytes 786448 | tf_op jit(solution)/shard_map/reduce_scatter | solution.py:126
  (154 shorter events, 41.6 us)
Async XLA Ops:
  6.5 21.4 %copy-start = (bf16[768,384]{1,0:T(8,128)(2,1)S(1)}, bf16[768,384]{1,0:T(8,128)(2,1)}, u32[]{:S(2)}) copy-start(bf16[768,384]{1,0:T(8,128)(2,1)} %param.16) | copy-start | bytes 1769476
  6.5 49.3 %copy-start.4 = (s32[6,1,4,2]{0,3,2,1:T(2,128)S(1)}, s32[6,1,4,2]{0,3,2,1:T(2,128)}, u32[]{:S(2)}) copy-start(s32[6,1,4,2]{0,3,2,1:T(2,128)} %param.18) | copy-start | bytes 580
  6.5 50.0 %copy-start.5 = (s32[6,1,4]{0,2,1:T(4,128)S(1)}, s32[6,1,4]{0,2,1:T(4,128)}, u32[]{:S(2)}) copy-start(s32[6,1,4]{0,2,1:T(4,128)} %param.19) | copy-start | bytes 292
  8.2 7.9 %copy-start.6 = (s32[6]{0:T(128)}, s32[6]{0:T(128)S(1)}, u32[]{:S(2)}) copy-start(s32[6]{0:T(128)S(1)} %get-tuple-element.82) | copy-start | bytes 76
  12.3 3.8 %copy-start.3 = (s32[1024]{0:T(1024)}, s32[1024]{0:T(1024)S(1)}, u32[]{:S(2)}) copy-start(s32[1024]{0:T(1024)S(1)} %pad_clamp_fusion.1) | copy-start | bytes 12292
  20.7 16.4 %all-to-all-start = ((bf16[8,2,6144]{2,1,0:T(2,128)(2,1)}), bf16[8,2,6144]{2,1,0:T(2,128)(2,1)S(1)}, u32[]{:S(2)}, u32[]{:S(2)}) async-start(bf16[8,2,6144]{2,1,0:T(2,128)(2,1)} %reshape.257), calls=%async_computation | async-start | bytes 393216 | tf_op jit(solution)/shard_map/all_to_all | solution.py:96
  28.0 32.9 %collective-permute-start = (bf16[768,384]{1,0:T(8,128)(2,1)S(1)}, bf16[768,384]{1,0:T(8,128)(2,1)S(1)}, u32[]{:S(2)}, u32[]{:S(2)}) collective-permute-start(bf16[768,384]{1,0:T(8,128)(2,1)S(1)} %copy-done), channel_id=1, source_target_pairs={{0,2},{2,4},{4,6},{6,8},{8,10},{10,12},{12,14},{14,0},{1,3},{3,5},... | collective-permute-start | bytes 1769480 | tf_op jit(solution)/shard_map/ppermute | solution.py:18
  37.1 23.8 %all-to-all-start.1 = ((bf16[8,2,6144]{2,1,0:T(2,128)(2,1)}), bf16[8,2,6144]{2,1,0:T(2,128)(2,1)S(1)}, u32[]{:S(2)}, u32[]{:S(2)}) async-start(bf16[8,2,6144]{2,1,0:T(2,128)(2,1)} %reshape.259), calls=%async_computation.1 | async-start | bytes 393216 | tf_op jit(solution)/shard_map/all_to_all | solution.py:97
  51.1 51.6 %collective-permute-start.4 = (bf16[768,384]{1,0:T(8,128)(2,1)S(1)}, bf16[768,384]{1,0:T(8,128)(2,1)S(1)}, u32[]{:S(2)}, u32[]{:S(2)}) collective-permute-start(bf16[768,384]{1,0:T(8,128)(2,1)S(1)} %copy-done), channel_id=1, source_target_pairs={{0,14},{2,0},{4,2},{6,4},{8,6},{10,8},{12,10},{14,12},{1,15},{3,1}... | collective-permute-start | bytes 1769480 | tf_op jit(solution)/shard_map/ppermute | solution.py:21
  55.9 11.7 %copy-start.2 = (s32[6,4,2]{1,2,0:T(2,128)}, s32[6,4,2]{1,2,0:T(2,128)S(1)}, u32[]{:S(2)}) copy-start(s32[6,4,2]{1,2,0:T(2,128)S(1)} %copy.100) | copy-start | bytes 580
  60.9 25.2 %collective-permute-start.1 = (bf16[768,384]{1,0:T(8,128)(2,1)S(1)}, bf16[768,384]{1,0:T(8,128)(2,1)S(1)}, u32[]{:S(2)}, u32[]{:S(2)}) collective-permute-start(bf16[768,384]{1,0:T(8,128)(2,1)S(1)} %collective-permute-done), channel_id=1, source_target_pairs={{0,2},{2,4},{4,6},{6,8},{8,10},{10,12},{12,14},{14,0},{1,3},{3,5},... | collective-permute-start | bytes 1769480 | tf_op jit(solution)/shard_map/ppermute | solution.py:18
  60.9 24.0 %all-to-all-start.2 = ((bf16[8,2,6144]{2,1,0:T(2,128)(2,1)}), bf16[8,2,6144]{2,1,0:T(2,128)(2,1)S(1)}, u32[]{:S(2)}, u32[]{:S(2)}) async-start(bf16[8,2,6144]{2,1,0:T(2,128)(2,1)} %reshape.261), calls=%async_computation.2 | async-start | bytes 393216 | tf_op jit(solution)/shard_map/all_to_all | solution.py:98
  78.9 5.0 %copy-start.1 = (bf16[3,256,128]{2,1,0:T(8,128)(2,1)}, bf16[3,256,128]{2,1,0:T(8,128)(2,1)S(1)}, u32[]{:S(2)}) copy-start(bf16[3,256,128]{2,1,0:T(8,128)(2,1)S(1)} %get-tuple-element.84) | copy-start | bytes 589828
  83.2 5.0 %copy-start.7 = (s32[6]{0:T(128)}, s32[6]{0:T(128)S(1)}, u32[]{:S(2)}) copy-start(s32[6]{0:T(128)S(1)} %get-tuple-element.83) | copy-start | bytes 76
  86.1 21.3 %collective-permute-start.2 = (bf16[768,384]{1,0:T(8,128)(2,1)S(1)}, bf16[768,384]{1,0:T(8,128)(2,1)S(1)}, u32[]{:S(2)}, u32[]{:S(2)}) collective-permute-start(bf16[768,384]{1,0:T(8,128)(2,1)S(1)} %collective-permute-done.1), channel_id=1, source_target_pairs={{0,2},{2,4},{4,6},{6,8},{8,10},{10,12},{12,14},{14,0},{1,3},{3,5},... | collective-permute-start | bytes 1769480 | tf_op jit(solution)/shard_map/ppermute | solution.py:18
  96.9 12.5 %all-to-all-start.3 = ((bf16[8,32,384]{2,1,0:T(8,128)(2,1)}), bf16[8,32,384]{2,1,0:T(8,128)(2,1)}, u32[]{:S(2)}, u32[]{:S(2)}) async-start(bf16[8,32,384]{2,1,0:T(8,128)(2,1)} %reshape.144), calls=%async_computation.3 | async-start | bytes 393216 | tf_op jit(solution)/shard_map/all_to_all | solution.py:114
  101.4 53.2 %reduce-scatter.2.cloned.1.call-start = ((), (), s32[]{:S(2)}) async-start(), calls=%async_computation.5 | async-start | bytes 2359296 | tf_op jit(solution)/shard_map/reduce_scatter | solution.py:126
  102.7 23.2 %collective-permute-start.5 = (bf16[768,384]{1,0:T(8,128)(2,1)S(1)}, bf16[768,384]{1,0:T(8,128)(2,1)S(1)}, u32[]{:S(2)}, u32[]{:S(2)}) collective-permute-start(bf16[768,384]{1,0:T(8,128)(2,1)S(1)} %collective-permute-done.4), channel_id=1, source_target_pairs={{0,14},{2,0},{4,2},{6,4},{8,6},{10,8},{12,10},{14,12},{1,15},{3,1}... | collective-permute-start | bytes 1769480 | tf_op jit(solution)/shard_map/ppermute | solution.py:21
  107.4 19.9 %collective-permute-start.3 = (bf16[768,384]{1,0:T(8,128)(2,1)S(1)}, bf16[768,384]{1,0:T(8,128)(2,1)}, u32[]{:S(2)}, u32[]{:S(2)}) collective-permute-start(bf16[768,384]{1,0:T(8,128)(2,1)S(1)} %collective-permute-done.2), channel_id=1, source_target_pairs={{0,2},{2,4},{4,6},{6,8},{8,10},{10,12},{12,14},{14,0},{1,3},{3,5},... | collective-permute-start | bytes 1769480 | tf_op jit(solution)/shard_map/ppermute | solution.py:18
  125.9 14.3 %collective-permute-start.6 = (bf16[768,384]{1,0:T(8,128)(2,1)S(1)}, bf16[768,384]{1,0:T(8,128)(2,1)S(1)}, u32[]{:S(2)}, u32[]{:S(2)}) collective-permute-start(bf16[768,384]{1,0:T(8,128)(2,1)S(1)} %collective-permute-done.5), channel_id=1, source_target_pairs={{0,14},{2,0},{4,2},{6,4},{8,6},{10,8},{12,10},{14,12},{1,15},{3,1}... | collective-permute-start | bytes 1769480 | tf_op jit(solution)/shard_map/ppermute | solution.py:21
Sparse Core Ops, SparseCore 0:
  145.9 8.6 reduce-scatter.1
